TPU v7x, 32 devices: a whole 2x2x4 slice. The times are simulated.
32 devices in a mesh: dir: 2 (over x), sx: 4 (over y, core), sy: 4 (over z).
Axes of the slice: x: 2, y: 2, z: 4, core: 2. Of those that a mesh axis runs over, the one named last changes fastest.
Arguments:
- signs_x: int32 [2, 256], P('dir', 'sx'), may hold values from -2147483648 to 2147483647, as said below
- signs_y: int32 [2, 512], P('dir', 'sy'), may hold values from -2147483648 to 2147483647, as said below
- heights: int32 [256, 512], P('sx', 'sy'), may hold values from 0 to 63
- velocity: float32 [256, 512], P('sx', 'sy'), may hold values from 1 to 2
- background: float32 [2, 256, 512], P('dir', 'sx', 'sy'), may hold values from -4 to 4
Outputs:
- basis: float32 [64, 256, 512], P('dir', 'sx', 'sy')
- factor: float32 [64, 64], P('dir')
Inputs may be any that keep to these rules, and one draw needn't show every extreme that they name: `signs_x`: packed sign words, every bit pattern possible. `signs_y`: packed sign words, every bit pattern possible.
All inputs are finite; a program needn't handle non-finite values.
Results may differ from a plain program's by a relative error of at most 0.00027.
Values sent between devices are 32-bit elements; how exact they have to be, the bound alone decides.
A program may use at most 64 MiB of HBM per device.

v0:
```python
import math

import jax
import jax.numpy as jnp
from jax import lax
from jax.sharding import PartitionSpec as P

PROBES = 32
LEVELS = 64


tau_step = 0.02


def with_halo(cells, sides, width):
    for axis, dim in sides:
        count = lax.axis_size(axis)
        ends = count - 1
        head = lax.slice_in_dim(cells, 0, width, axis=dim)
        tail = lax.slice_in_dim(cells, cells.shape[dim] - width, cells.shape[dim], axis=dim)
        cells = jnp.concatenate(
            [
                lax.ppermute(tail, axis, [(i, (i + 1) % count) for i in range(ends)]),
                cells,
                lax.ppermute(head, axis, [((i + 1) % count, i) for i in range(ends)]),
            ],
            axis=dim,
        )
    return cells


def unpack_signs(packed, per_group):
    bit_index = jnp.arange(per_group, dtype=jnp.int32)
    bit_values = jnp.right_shift(packed[:, None, :], bit_index[None, :, None]) & 1
    signed = (2 * bit_values - 1).astype(jnp.float32)
    return signed.reshape(packed.shape[0] * per_group, packed.shape[1])


def apply_step(wavefield, stiffness):
    weighted = stiffness * wavefield
    padded = with_halo(weighted, (("sx", 1), ("sy", 2)), 1)
    laplace = (
        padded[:, 2:, 1:-1]
        + padded[:, :-2, 1:-1]
        + padded[:, 1:-1, 2:]
        + padded[:, 1:-1, :-2]
        - 4.0 * weighted
    )
    return wavefield + tau_step * stiffness * laplace


def responses_for(signs_first, signs_second, shot_data, stiffness):
    first_signs = unpack_signs(signs_first, PROBES)
    second = unpack_signs(signs_second, PROBES)
    kronecker = first_signs[:, :, None] * second[:, None, :]
    groups = shot_data.shape[0]
    rows_x = shot_data.shape[1]
    rows_y = shot_data.shape[2]
    rolled = jnp.roll(kronecker.reshape(groups, PROBES, rows_x, rows_y), -1, axis=1).reshape(
        kronecker.shape
    )
    probe_dirs = kronecker + 0.5 * rolled
    shot_fields = jnp.repeat(shot_data, PROBES, axis=0)
    wavefield = shot_fields * probe_dirs
    for repeat in range(4):
        wavefield = apply_step(wavefield, stiffness[None])
    return (shot_fields * wavefield).reshape(groups * PROBES, rows_x * rows_y)


def shards(signs_x, signs_y, heights, velocity, background):
    rows_x = background.shape[1]
    rows_y = background.shape[2]
    stiffness = velocity * jnp.sqrt(1.0 + heights.astype(jnp.float32) / LEVELS)
    response = responses_for(signs_x, signs_y, background, stiffness)
    all_rows = lax.all_gather(response, "dir", axis=0, tiled=True)
    local_gram = jnp.dot(
        all_rows, all_rows.T, precision=lax.Precision.HIGHEST, preferred_element_type=jnp.float32
    )
    gram_matrix = lax.psum(local_gram, ("sx", "sy"))
    factor_low = jnp.linalg.cholesky(gram_matrix)
    orthonormal = lax.linalg.triangular_solve(factor_low, all_rows, left_side=True, lower=True)
    factor_r = factor_low.T
    cell_count = math.sqrt(rows_x * rows_y * lax.axis_size("sx") * lax.axis_size("sy"))
    row_start = lax.axis_index("dir") * PROBES
    own_q = lax.dynamic_slice_in_dim(orthonormal, row_start, PROBES, 0)
    own_r = lax.dynamic_slice_in_dim(factor_r, row_start, PROBES, 0)
    basis = (own_q * cell_count).reshape(PROBES, rows_x, rows_y)
    factor = own_r / cell_count
    return (basis, factor)


def solution(mesh):
    in_specs = (P("dir", "sx"), P("dir", "sy"), P("sx", "sy"), P("sx", "sy"), P("dir", "sx", "sy"))
    out_specs = (P("dir", "sx", "sy"), P("dir", None))
    return jax.shard_map(shards, mesh=mesh, in_specs=in_specs, out_specs=out_specs, check_vma=False)
```

profile of v0, /device:TPU:0, one launch (start us, length us, event | category | flops | bytes accessed | tf_op | source)
XLA Modules:
  0.0 231.4 jit_solution(7985730447501686642)
XLA Ops:
  7.2 0.7 add_convert_fusion
  7.9 0.7 add_convert_fusion.1
  8.6 0.3 broadcast_multiply_fusion.3
  9.0 0.1 slice.164
  9.2 0.5 copy-done.3
  9.8 0.4 fusion.29
  10.2 1.3 collective-permute-start
  11.5 3.0 %collective-permute-start.1 = (f32[32,1,128]{2,0,1:T(8,128)S(1)}, f32[32,1,128]{2,0,1:T(8,128)S(1)}, u32[]{:S(2)}, u32[]{:S(2)}) collective-permute-start(f32[32,1,128]{2,0,1:T(8,128)S(1)} %get-tuple-element.34), channel_id=1, source_target_pairs={{0,4},{4,8},{8,12},{1,5},{5,9},{9,13},{2,6},{6,10},{10,14},{3,7},{... | collective-permute-start | bytes 49160 | tf_op jit(solution)/shard_map/ppermute | solution.py:23
  14.5 0.8 collective-permute-done.1
  15.4 1.8 fusion.39
  17.1 1.9 copy.23
  19.0 1.3 collective-permute-start.2
  20.3 1.9 copy.25
  22.2 5.6 %collective-permute-start.3 = (f32[32,66,1]{1,0,2:T(8,128)S(1)}, f32[32,66,1]{1,0,2:T(8,128)S(1)}, u32[]{:S(2)}, u32[]{:S(2)}) collective-permute-start(f32[32,66,1]{1,0,2:T(8,128)S(1)} %copy.25), channel_id=1, source_target_pairs={{0,1},{1,2},{2,3},{4,5},{5,6},{6,7},{8,9},{9,10},{10,11},{12,13},{... | collective-permute-start | bytes 25352 | tf_op jit(solution)/shard_map/ppermute | solution.py:23
  27.7 1.9 copy.24
  29.6 1.9 copy.26
  31.6 3.9 %broadcast_multiply_fusion.2 = (f32[32,64,128]{2,0,1:T(8,128)S(1)}, f32[32,64,128]{2,0,1:T(8,128)}) fusion(f32[64,128]{1,0:T(8,128)S(1)} %get-tuple-element.19, f32[32,64,128]{2,0,1:T(8,128)S(1)} %fusion.29, f32[32,1,128]{2,0,1:T(8,128)S(1)} %collective-permute-done, f32[32,1,128]{2,0,1:T(8,128)S(1)} %collective-permute-done.1, f32[32,66,1]{2,0,1:T(8,128)} %copy.26, ...), kind=kLoop, calls=%fused_computation.71 | loop fusion | flops 5505024 | bytes 4366848 | tf_op jit(solution)/shard_map/mul | solution.py:40
  35.5 1.3 collective-permute-start.4
  36.8 3.6 %collective-permute-start.5 = (f32[32,1,128]{2,0,1:T(8,128)S(1)}, f32[32,1,128]{2,0,1:T(8,128)S(1)}, u32[]{:S(2)}, u32[]{:S(2)}) collective-permute-start(f32[32,1,128]{2,0,1:T(8,128)S(1)} %get-tuple-element.32), channel_id=1, source_target_pairs={{0,4},{4,8},{8,12},{1,5},{5,9},{9,13},{2,6},{6,10},{10,14},{3,7},{... | collective-permute-start | bytes 49160 | tf_op jit(solution)/shard_map/ppermute | solution.py:23
  40.3 0.8 collective-permute-done.5
  41.2 1.4 fusion.38
  42.6 1.9 copy.27
  44.5 1.3 collective-permute-start.6
  45.8 0.7 copy.29
  46.5 4.5 %collective-permute-start.7 = (f32[32,66,1]{1,0,2:T(8,128)S(1)}, f32[32,66,1]{1,0,2:T(8,128)S(1)}, u32[]{:S(2)}, u32[]{:S(2)}) collective-permute-start(f32[32,66,1]{1,0,2:T(8,128)S(1)} %copy.29), channel_id=1, source_target_pairs={{0,1},{1,2},{2,3},{4,5},{5,6},{6,7},{8,9},{9,10},{10,11},{12,13},{... | collective-permute-start | bytes 25352 | tf_op jit(solution)/shard_map/ppermute | solution.py:23
  51.0 1.1 copy.28
  52.1 0.3 collective-permute-done.7
  52.5 1.9 copy.30
  54.4 3.4 %broadcast_multiply_fusion.1 = (f32[32,64,128]{2,0,1:T(8,128)S(1)}, f32[32,64,128]{2,0,1:T(8,128)}) fusion(f32[64,128]{1,0:T(8,128)S(1)} %get-tuple-element.19, f32[32,64,128]{2,0,1:T(8,128)} %get-tuple-element.17, f32[32,64,128]{2,0,1:T(8,128)S(1)} %get-tuple-element.16, f32[32,1,128]{2,0,1:T(8,128)S(1)} %collective-permute-done.4, ...), kind=kLoop, calls=%fused_computation.70 | loop fusion | flops 4194304 | bytes 4309504 | tf_op jit(solution)/shard_map/mul | solution.py:40
  57.8 1.3 collective-permute-start.8
  59.1 4.6 %collective-permute-start.9 = (f32[32,1,128]{2,0,1:T(8,128)S(1)}, f32[32,1,128]{2,0,1:T(8,128)S(1)}, u32[]{:S(2)}, u32[]{:S(2)}) collective-permute-start(f32[32,1,128]{2,0,1:T(8,128)S(1)} %get-tuple-element.30), channel_id=1, source_target_pairs={{0,4},{4,8},{8,12},{1,5},{5,9},{9,13},{2,6},{6,10},{10,14},{3,7},{... | collective-permute-start | bytes 49160 | tf_op jit(solution)/shard_map/ppermute | solution.py:23
  63.7 0.8 collective-permute-done.9
  64.6 0.4 fusion.37
  64.9 0.7 copy.31
  65.7 1.3 collective-permute-start.10
  67.0 0.7 copy.33
  67.7 4.7 %collective-permute-start.11 = (f32[32,66,1]{1,0,2:T(8,128)S(1)}, f32[32,66,1]{1,0,2:T(8,128)S(1)}, u32[]{:S(2)}, u32[]{:S(2)}) collective-permute-start(f32[32,66,1]{1,0,2:T(8,128)S(1)} %copy.33), channel_id=1, source_target_pairs={{0,1},{1,2},{2,3},{4,5},{5,6},{6,7},{8,9},{9,10},{10,11},{12,13},{... | collective-permute-start | bytes 25352 | tf_op jit(solution)/shard_map/ppermute | solution.py:23
  72.4 1.1 copy.32
  73.5 0.2 collective-permute-done.11
  73.7 1.9 copy.34
  75.6 3.4 %broadcast_multiply_fusion = (f32[32,64,128]{2,0,1:T(8,128)S(1)}, f32[32,64,128]{2,0,1:T(8,128)}) fusion(f32[64,128]{1,0:T(8,128)S(1)} %get-tuple-element.19, f32[32,64,128]{2,0,1:T(8,128)} %get-tuple-element.15, f32[32,64,128]{2,0,1:T(8,128)S(1)} %get-tuple-element.14, f32[32,1,128]{2,0,1:T(8,128)S(1)} %collective-permute-done.8, ...), kind=kLoop, calls=%fused_computation.69 | loop fusion | flops 4194304 | bytes 4309504 | tf_op jit(solution)/shard_map/mul | solution.py:40
  79.0 1.3 collective-permute-start.12
  80.3 5.5 %collective-permute-start.13 = (f32[32,1,128]{2,0,1:T(8,128)S(1)}, f32[32,1,128]{2,0,1:T(8,128)S(1)}, u32[]{:S(2)}, u32[]{:S(2)}) collective-permute-start(f32[32,1,128]{2,0,1:T(8,128)S(1)} %get-tuple-element.28), channel_id=1, source_target_pairs={{0,4},{4,8},{8,12},{1,5},{5,9},{9,13},{2,6},{6,10},{10,14},{3,7},{... | collective-permute-start | bytes 49160 | tf_op jit(solution)/shard_map/ppermute | solution.py:23
  85.8 0.8 collective-permute-done.13
  86.7 1.4 fusion.36
  88.1 1.9 copy.35
  89.9 1.3 collective-permute-start.14
  91.2 0.7 copy.37
  91.9 4.7 %collective-permute-start.15 = (f32[32,66,1]{1,0,2:T(8,128)S(1)}, f32[32,66,1]{1,0,2:T(8,128)S(1)}, u32[]{:S(2)}, u32[]{:S(2)}) collective-permute-start(f32[32,66,1]{1,0,2:T(8,128)S(1)} %copy.37), channel_id=1, source_target_pairs={{0,1},{1,2},{2,3},{4,5},{5,6},{6,7},{8,9},{9,10},{10,11},{12,13},{... | collective-permute-start | bytes 25352 | tf_op jit(solution)/shard_map/ppermute | solution.py:23
  96.6 1.1 copy.36
  97.7 0.3 collective-permute-done.15
  98.1 1.9 copy.38
  100.0 3.1 %copy_bitcast_fusion = f32[32,8192]{1,0:T(8,128)} fusion(f32[32,64,128]{2,0,1:T(8,128)S(1)} %copy-done.1, f32[32,66,1]{2,0,1:T(8,128)} %copy.38, f32[32,1,128]{2,0,1:T(8,128)S(1)} %collective-permute-done.12, f32[32,64,128]{2,0,1:T(8,128)S(1)} %get-tuple-element.12, f32[32,1,128]{2,0,1:T(8,128)S(1)} %collective-permute-done.13, f32[32,66,1]{2,0,1:T(8,128)S(1)} %copy.36, ...), kind=kLoop, calls=%fused_computation.4 | loop fusion | flops 4194304 | bytes 3260928 | tf_op jit(solution)/shard_map/reshape | solution.py:67
  103.1 39.8 %all-gather.2.cloned.1.call-done = f32[64,8192]{1,0:T(8,128)} async-done(((f32[32,8192]{1,0:T(8,128)}), f32[64,8192]{1,0:T(8,128)}) %all-gather.2.cloned.1.call-update) | async-done | bytes 2097168 | tf_op jit(solution)/shard_map/all_gather | solution.py:75
  142.9 4.2 %fusion.44 = f32[64,64]{0,1:T(8,128)S(1)} fusion(f32[64,8192]{1,0:T(8,128)} %all-gather.2.cloned.1.call-done), kind=kOutput, calls=%fused_computation.96 | convolution fusion | flops 402653184 | bytes 2113536 | tf_op jit(solution)/shard_map/dot_general | solution.py:76
  147.1 61.3 %psum.7 = f32[64,64]{0,1:T(8,128)S(1)} all-reduce(f32[64,64]{0,1:T(8,128)S(1)} %fusion.44), channel_id=1, replica_groups=mesh['dir'=2,'sx'=4,'sy'=4] {'sx','sy'}, use_global_device_ids=true, to_apply=%region_0.1 | all-reduce | flops 4096 | bytes 32768 | tf_op jit(solution)/shard_map/psum | solution.py:79
  208.5 5.8 %cholesky.16 = f32[64,64]{1,0:T(8,128)S(1)} custom-call(f32[64,64]{1,0:T(8,128)S(1)} %fusion.32), custom_call_target="Cholesky" | custom-call | tf_op jit(solution)/shard_map/jit(cholesky)/cholesky | solution.py:80
  214.3 0.6 compare_reduce_fusion
  215.0 0.7 select_bitcast_fusion
  215.7 4.9 %custom-call.6 = f32[1,64,64]{1,2,0:T(8,128)S(1)} custom-call(f32[1,64,64]{2,1,0:T(8,128)S(1)} %get-tuple-element.10), custom_call_target="InvertDiagBlocksLowerTriangular" | custom-call | tf_op jit(solution)/shard_map/triangular_solve | solution.py:81
  220.6 1.9 fusion.30
  222.5 0.1 multiply_bitcast_fusion
  222.6 1.2 copy.45
  223.8 0.7 copy.42
  (34 shorter events, 0.7 us)
Async XLA Ops:
  7.2 135.7 %all-gather.2.cloned.1.call-start = ((), (), s32[]{:S(2)}) async-start(), calls=%async_computation | async-start | bytes 3145728 | tf_op jit(solution)/shard_map/all_gather | solution.py:75
  9.0 0.8 copy-start.3
  9.0 0.8 copy-start.4
  9.0 0.8 copy-start.2
  10.2 4.3 %collective-permute-start = (f32[32,1,128]{2,0,1:T(8,128)S(1)}, f32[32,1,128]{2,0,1:T(8,128)S(1)}, u32[]{:S(2)}, u32[]{:S(2)}) collective-permute-start(f32[32,1,128]{2,0,1:T(8,128)S(1)} %get-tuple-element.35), channel_id=1, source_target_pairs={{4,0},{8,4},{12,8},{5,1},{9,5},{13,9},{6,2},{10,6},{14,10},{7,3},{... | collective-permute-start | bytes 49160 | tf_op jit(solution)/shard_map/ppermute | solution.py:25
  11.5 3.9 %collective-permute-start.1 = (f32[32,1,128]{2,0,1:T(8,128)S(1)}, f32[32,1,128]{2,0,1:T(8,128)S(1)}, u32[]{:S(2)}, u32[]{:S(2)}) collective-permute-start(f32[32,1,128]{2,0,1:T(8,128)S(1)} %get-tuple-element.34), channel_id=1, source_target_pairs={{0,4},{4,8},{8,12},{1,5},{5,9},{9,13},{2,6},{6,10},{10,14},{3,7},{... | collective-permute-start | bytes 49160 | tf_op jit(solution)/shard_map/ppermute | solution.py:23
  19.0 8.7 %collective-permute-start.2 = (f32[32,66,1]{1,0,2:T(8,128)S(1)}, f32[32,66,1]{1,0,2:T(8,128)S(1)}, u32[]{:S(2)}, u32[]{:S(2)}) collective-permute-start(f32[32,66,1]{1,0,2:T(8,128)S(1)} %copy.23), channel_id=1, source_target_pairs={{1,0},{2,1},{3,2},{5,4},{6,5},{7,6},{9,8},{10,9},{11,10},{13,12},{... | collective-permute-start | bytes 25352 | tf_op jit(solution)/shard_map/ppermute | solution.py:25
  22.2 7.5 %collective-permute-start.3 = (f32[32,66,1]{1,0,2:T(8,128)S(1)}, f32[32,66,1]{1,0,2:T(8,128)S(1)}, u32[]{:S(2)}, u32[]{:S(2)}) collective-permute-start(f32[32,66,1]{1,0,2:T(8,128)S(1)} %copy.25), channel_id=1, source_target_pairs={{0,1},{1,2},{2,3},{4,5},{5,6},{6,7},{8,9},{9,10},{10,11},{12,13},{... | collective-permute-start | bytes 25352 | tf_op jit(solution)/shard_map/ppermute | solution.py:23
  35.5 4.9 %collective-permute-start.4 = (f32[32,1,128]{2,0,1:T(8,128)S(1)}, f32[32,1,128]{2,0,1:T(8,128)S(1)}, u32[]{:S(2)}, u32[]{:S(2)}) collective-permute-start(f32[32,1,128]{2,0,1:T(8,128)S(1)} %get-tuple-element.33), channel_id=1, source_target_pairs={{4,0},{8,4},{12,8},{5,1},{9,5},{13,9},{6,2},{10,6},{14,10},{7,3},{... | collective-permute-start | bytes 49160 | tf_op jit(solution)/shard_map/ppermute | solution.py:25
  36.8 4.4 %collective-permute-start.5 = (f32[32,1,128]{2,0,1:T(8,128)S(1)}, f32[32,1,128]{2,0,1:T(8,128)S(1)}, u32[]{:S(2)}, u32[]{:S(2)}) collective-permute-start(f32[32,1,128]{2,0,1:T(8,128)S(1)} %get-tuple-element.32), channel_id=1, source_target_pairs={{0,4},{4,8},{8,12},{1,5},{5,9},{9,13},{2,6},{6,10},{10,14},{3,7},{... | collective-permute-start | bytes 49160 | tf_op jit(solution)/shard_map/ppermute | solution.py:23
  44.5 6.6 %collective-permute-start.6 = (f32[32,66,1]{1,0,2:T(8,128)S(1)}, f32[32,66,1]{1,0,2:T(8,128)S(1)}, u32[]{:S(2)}, u32[]{:S(2)}) collective-permute-start(f32[32,66,1]{1,0,2:T(8,128)S(1)} %copy.27), channel_id=1, source_target_pairs={{1,0},{2,1},{3,2},{5,4},{6,5},{7,6},{9,8},{10,9},{11,10},{13,12},{... | collective-permute-start | bytes 25352 | tf_op jit(solution)/shard_map/ppermute | solution.py:25
  46.5 6.0 %collective-permute-start.7 = (f32[32,66,1]{1,0,2:T(8,128)S(1)}, f32[32,66,1]{1,0,2:T(8,128)S(1)}, u32[]{:S(2)}, u32[]{:S(2)}) collective-permute-start(f32[32,66,1]{1,0,2:T(8,128)S(1)} %copy.29), channel_id=1, source_target_pairs={{0,1},{1,2},{2,3},{4,5},{5,6},{6,7},{8,9},{9,10},{10,11},{12,13},{... | collective-permute-start | bytes 25352 | tf_op jit(solution)/shard_map/ppermute | solution.py:23
  57.8 5.9 %collective-permute-start.8 = (f32[32,1,128]{2,0,1:T(8,128)S(1)}, f32[32,1,128]{2,0,1:T(8,128)S(1)}, u32[]{:S(2)}, u32[]{:S(2)}) collective-permute-start(f32[32,1,128]{2,0,1:T(8,128)S(1)} %get-tuple-element.31), channel_id=1, source_target_pairs={{4,0},{8,4},{12,8},{5,1},{9,5},{13,9},{6,2},{10,6},{14,10},{7,3},{... | collective-permute-start | bytes 49160 | tf_op jit(solution)/shard_map/ppermute | solution.py:25
  59.1 5.4 %collective-permute-start.9 = (f32[32,1,128]{2,0,1:T(8,128)S(1)}, f32[32,1,128]{2,0,1:T(8,128)S(1)}, u32[]{:S(2)}, u32[]{:S(2)}) collective-permute-start(f32[32,1,128]{2,0,1:T(8,128)S(1)} %get-tuple-element.30), channel_id=1, source_target_pairs={{0,4},{4,8},{8,12},{1,5},{5,9},{9,13},{2,6},{6,10},{10,14},{3,7},{... | collective-permute-start | bytes 49160 | tf_op jit(solution)/shard_map/ppermute | solution.py:23
  65.7 6.7 %collective-permute-start.10 = (f32[32,66,1]{1,0,2:T(8,128)S(1)}, f32[32,66,1]{1,0,2:T(8,128)S(1)}, u32[]{:S(2)}, u32[]{:S(2)}) collective-permute-start(f32[32,66,1]{1,0,2:T(8,128)S(1)} %copy.31), channel_id=1, source_target_pairs={{1,0},{2,1},{3,2},{5,4},{6,5},{7,6},{9,8},{10,9},{11,10},{13,12},{... | collective-permute-start | bytes 25352 | tf_op jit(solution)/shard_map/ppermute | solution.py:25
  67.7 6.0 %collective-permute-start.11 = (f32[32,66,1]{1,0,2:T(8,128)S(1)}, f32[32,66,1]{1,0,2:T(8,128)S(1)}, u32[]{:S(2)}, u32[]{:S(2)}) collective-permute-start(f32[32,66,1]{1,0,2:T(8,128)S(1)} %copy.33), channel_id=1, source_target_pairs={{0,1},{1,2},{2,3},{4,5},{5,6},{6,7},{8,9},{9,10},{10,11},{12,13},{... | collective-permute-start | bytes 25352 | tf_op jit(solution)/shard_map/ppermute | solution.py:23
  79.0 6.8 %collective-permute-start.12 = (f32[32,1,128]{2,0,1:T(8,128)S(1)}, f32[32,1,128]{2,0,1:T(8,128)S(1)}, u32[]{:S(2)}, u32[]{:S(2)}) collective-permute-start(f32[32,1,128]{2,0,1:T(8,128)S(1)} %get-tuple-element.29), channel_id=1, source_target_pairs={{4,0},{8,4},{12,8},{5,1},{9,5},{13,9},{6,2},{10,6},{14,10},{7,3},{... | collective-permute-start | bytes 49160 | tf_op jit(solution)/shard_map/ppermute | solution.py:25
  80.3 6.4 %collective-permute-start.13 = (f32[32,1,128]{2,0,1:T(8,128)S(1)}, f32[32,1,128]{2,0,1:T(8,128)S(1)}, u32[]{:S(2)}, u32[]{:S(2)}) collective-permute-start(f32[32,1,128]{2,0,1:T(8,128)S(1)} %get-tuple-element.28), channel_id=1, source_target_pairs={{0,4},{4,8},{8,12},{1,5},{5,9},{9,13},{2,6},{6,10},{10,14},{3,7},{... | collective-permute-start | bytes 49160 | tf_op jit(solution)/shard_map/ppermute | solution.py:23
  89.9 6.7 %collective-permute-start.14 = (f32[32,66,1]{1,0,2:T(8,128)S(1)}, f32[32,66,1]{1,0,2:T(8,128)S(1)}, u32[]{:S(2)}, u32[]{:S(2)}) collective-permute-start(f32[32,66,1]{1,0,2:T(8,128)S(1)} %copy.35), channel_id=1, source_target_pairs={{1,0},{2,1},{3,2},{5,4},{6,5},{7,6},{9,8},{10,9},{11,10},{13,12},{... | collective-permute-start | bytes 25352 | tf_op jit(solution)/shard_map/ppermute | solution.py:25
  91.9 8.0 %copy-start.1 = (f32[32,64,128]{2,0,1:T(8,128)S(1)}, f32[32,64,128]{2,0,1:T(8,128)}, u32[]{:S(2)}) copy-start(f32[32,64,128]{2,0,1:T(8,128)} %get-tuple-element.13) | copy-start | bytes 3145732
  91.9 6.1 %collective-permute-start.15 = (f32[32,66,1]{1,0,2:T(8,128)S(1)}, f32[32,66,1]{1,0,2:T(8,128)S(1)}, u32[]{:S(2)}, u32[]{:S(2)}) collective-permute-start(f32[32,66,1]{1,0,2:T(8,128)S(1)} %copy.37), channel_id=1, source_target_pairs={{0,1},{1,2},{2,3},{4,5},{5,6},{6,7},{8,9},{9,10},{10,11},{12,13},{... | collective-permute-start | bytes 25352 | tf_op jit(solution)/shard_map/ppermute | solution.py:23
  142.9 77.7 %copy-start = (f32[64,8192]{1,0:T(8,128)S(1)}, f32[64,8192]{1,0:T(8,128)}, u32[]{:S(2)}) copy-start(f32[64,8192]{1,0:T(8,128)} %all-gather.2.cloned.1.call-done) | copy-start | bytes 6291460
Sparse Core Ops, SparseCore 0:
  103.2 39.6 all-gather.1
where the time goes:
time: 232 us; the launch traced here: 231 us
  blocking collectives  61.3 us (26%)
  starting transfers between devices  46.5 us (20%)
  waiting for transfers between devices  43.9 us (19%)
  local copies, waits for them, and re-layouts  30.7 us (13%)
  other arithmetic  28.4 us (12%)
  between operations  14.4 us (6%)
  matrix products  6.09 us (3%)
    psum x1, blocking collectives, shards(): gram_matrix = lax.psum(local_gram, ('sx', 'sy'))  61.3 us
    all_gather x1, waiting for transfers between devices, shards(): all_rows = lax.all_gather(response, 'dir', axis=0, tiled=True)  39.8 us
    ppermute x8, starting transfers between devices, with_halo(): lax.ppermute(tail, axis, [(i, (i + 1) % count) for i in range(ends)])  36.2 us
    slice x8, local copies, waits for them, and re-layouts, with_halo(): head = lax.slice_in_dim(cells, 0, width, axis=dim)  11.2 us
    mul x4, other arithmetic, apply_step(): weighted = stiffness * wavefield  11 us
    ppermute x8, starting transfers between devices, with_halo(): lax.ppermute(head, axis, [((i + 1) % count, i) for i in range(ends)])  10.3 us
    ppermute x4, local copies, waits for them, and re-layouts, with_halo(): lax.ppermute(tail, axis, [(i, (i + 1) % count) for i in range(ends)])  7.68 us
    another operation x3, other arithmetic, shards(): factor_low = jnp.linalg.cholesky(gram_matrix)  6.52 us
  transfers between devices with their start and end apart: 17, of which 8 were waited for; matrix products, arithmetic and copies ran while one was open for 4% of the time, Pallas kernels for 0%

commit v1 on v0

v1 whole, which is shorter than its diff:
```python
import functools
import math

import jax
import jax.numpy as jnp
from jax import lax
from jax.experimental import pallas as pl
from jax.experimental.pallas import tpu as pltpu
from jax.sharding import PartitionSpec as P

PROBES = 32
LEVELS = 64
TAU = 0.02
STEPS = 4
SUB = 8
GROUP = 16
UNROLL = 4
MESH = pl.DeviceIdType.MESH
OFFS = [(dx, dy) for dx in (-1, 0, 1) for dy in (-1, 0, 1)]
SLOT = {o: n for n, o in enumerate(OFFS)}
HIGH = lax.Precision.HIGHEST
F32 = jnp.float32
BF16 = jnp.bfloat16


def kernel(S, NX, NY, X, Y, sx_ref, sy_ref, h_ref, v_ref, b_ref, out_ref, fac_ref,
           pk, rc, aext, qext, pext, cc, sxw, fy, fyn, rbuf, xb, gx, gy, aug,
           send_sem, recv_sem, gxs, gxr, gys, gyr):
    D = S * PROBES
    E = X + 2 * SUB
    md = lax.axis_index("dir")
    mx = lax.axis_index("sx")
    my = lax.axis_index("sy")
    lane8 = lax.broadcasted_iota(jnp.int32, (SUB, Y), 1)

    def conds(dx, dy):
        out = []
        for c, o, n in ((mx, dx, NX), (my, dy, NY)):
            if o > 0:
                out.append(c < n - o)
            elif o < 0:
                out.append(c >= -o)
        return out

    def there(dx, dy):
        flags = conds(dx, dy)
        return flags[0] if len(flags) == 1 else jnp.logical_and(*flags)

    def when(flags, f):
        if not flags:
            f()
        elif len(flags) == 1:
            pl.when(flags[0])(f)
        else:
            pl.when(flags[0])(lambda: when(flags[1:], f))

    def device(d, dx, dy):
        return (d, lax.rem(mx + (dx + NX), NX), lax.rem(my + (dy + NY), NY))

    def of_message(d, dx, dy):
        return [md != d] if (dx, dy) == (0, 0) else conds(dx, dy)

    barrier = pltpu.get_barrier_semaphore()
    count = jnp.int32(0)

    def greet(flags, d, dx, dy):
        when(flags, lambda: pl.semaphore_signal(
            barrier, inc=1, device_id=device(d, dx, dy), device_id_type=MESH))
        one = jnp.int32(1)
        for flag in flags:
            one = one * jnp.where(flag, 1, 0)
        return one

    for d in range(S):
        for dx, dy in OFFS:
            count += greet(of_message(d, dx, dy), d, dx, dy)
    for k in range(2, NX):
        for dx in (k, -k):
            count += greet(conds(dx, 0), md, dx, 0)
    for k in range(2, NY):
        for dy in (k, -k):
            count += greet(conds(0, dy), md, 0, dy)

    stiff = v_ref[...] * jnp.sqrt(1.0 + h_ref[...].astype(F32) / LEVELS)
    sq = stiff * stiff
    a = stiff * b_ref[0]
    q = TAU * sq
    SG, EW, NT, SG2, NB = X, X + 8, X + 16, X + 32, X + 40
    pk[0:X, :] = a
    for base in (SG, SG2):
        syv = sy_ref[...]
        sxv = sx_ref[...]
        pk[base:base + 1, :] = (syv >> 16).astype(F32)
        pk[base + 1:base + 2, :] = (syv & 0xFFFF).astype(F32)
        pk[base + 2:base + 3, 0:X] = (sxv >> 16).astype(F32)
        pk[base + 3:base + 4, 0:X] = (sxv & 0xFFFF).astype(F32)
    edge = jnp.zeros((SUB, Y), F32)
    for r in range(X // SUB):
        ar = a[r * SUB:(r + 1) * SUB]
        qr = q[r * SUB:(r + 1) * SUB]
        t = jnp.where(jnp.logical_or(lane8 < 4, lane8 >= Y - 4), ar,
                      jnp.where(lane8 < 8, pltpu.roll(qr, 4, 1), pltpu.roll(qr, Y - 4, 1)))
        t = pltpu.roll(t, (16 * r + 8) % Y, 1)
        edge = jnp.where((lane8 >> 4) == r, t, edge)
    pk[EW:EW + 8, :] = edge
    pk[NT:NT + 8, :] = a[0:8]
    pk[NT + 8:NT + 16, :] = q[0:8]
    pk[NB:NB + 8, :] = a[X - 8:X]
    pk[NB + 8:NB + 16, :] = q[X - 8:X]

    def parts(dx, dy):
        if (dx, dy) == (0, 0):
            return 0, X + 8
        if dy == 0:
            return (NT, 24) if dx < 0 else (SG2, 24)
        return SG, 16

    pl.semaphore_wait(barrier, count)

    def copy_to(d, dx, dy):
        start, rows = parts(dx, dy)
        return pltpu.make_async_remote_copy(
            src_ref=pk.at[pl.ds(start, rows)],
            dst_ref=rc.at[md * 9 + SLOT[(-dx, -dy)], pl.ds(0, rows)],
            send_sem=send_sem.at[d * 9 + SLOT[(dx, dy)]],
            recv_sem=recv_sem.at[md * 9 + SLOT[(-dx, -dy)]],
            device_id=device(d, dx, dy), device_id_type=MESH)

    def each_message(f):
        for d in range(S):
            for dx, dy in OFFS:
                when(of_message(d, dx, dy), functools.partial(f, d, dx, dy))

    each_message(lambda d, dx, dy: copy_to(d, dx, dy).start())
    rc[md * 9 + SLOT[(0, 0)], 0:X + 8, :] = pk[0:X + 8, :]

    def wait_recv(s, dx, dy):
        start, rows = parts(-dx, -dy)
        pltpu.make_async_remote_copy(
            src_ref=pk.at[pl.ds(start, rows)],
            dst_ref=rc.at[s * 9 + SLOT[(dx, dy)], pl.ds(0, rows)],
            send_sem=send_sem.at[s * 9 + SLOT[(dx, dy)]],
            recv_sem=recv_sem.at[s * 9 + SLOT[(dx, dy)]],
            device_id=device(s, dx, dy), device_id_type=MESH).wait_recv()

    each_message(wait_recv)
    each_message(lambda d, dx, dy: copy_to(d, dx, dy).wait_send())

    lane1 = lax.broadcasted_iota(jnp.int32, (1, Y), 1)
    jv = lax.broadcasted_iota(jnp.int32, (PROBES, 2 * Y), 0)

    def masked(ok, val):
        return jnp.where(ok, val, jnp.zeros_like(val))

    def words(s, slot, base, row):
        hi = rc[s * 9 + slot, base + row:base + row + 1, :].astype(jnp.int32)
        lo = rc[s * 9 + slot, base + row + 1:base + row + 2, :].astype(jnp.int32)
        return (hi << 16) | lo

    def halo(s, dx, r):
        out = []
        for dy in (1, -1):
            pack = rc[s * 9 + SLOT[(dx, dy)], 8:16, :]
            out.append(masked(there(dx, dy), pltpu.roll(pack, (-(16 * r + 8)) % Y, 1)))
        e, w = out
        zero = jnp.zeros_like(e)
        ha = jnp.where(lane8 < 4, e, jnp.where(lane8 >= Y - 4, w, zero))
        hq = jnp.where(lane8 < 4, pltpu.roll(e, Y - 4, 1),
                       jnp.where(lane8 >= Y - 4, pltpu.roll(w, 4, 1), zero))
        return ha, hq

    def put_q(rows, cols, val):
        qext[cols, rows] = val
        pext[cols, rows] = 1.0 - 4.0 * val

    lo_c, hi_c = 0, 1
    put_q(slice(SUB, SUB + X), lo_c, q)
    for s in range(S):
        nslot, sslot = SLOT[(-1, 0)], SLOT[(1, 0)]
        aext[s, lo_c, SUB:SUB + X] = rc[s * 9 + SLOT[(0, 0)], 0:X, :]
        aext[s, lo_c, 0:SUB] = masked(there(-1, 0), rc[s * 9 + nslot, 8:16, :])
        aext[s, lo_c, SUB + X:E] = masked(there(1, 0), rc[s * 9 + sslot, 0:8, :])
        if s == 0:
            put_q(slice(0, SUB), lo_c, masked(there(-1, 0), rc[s * 9 + nslot, 16:24, :]))
            put_q(slice(SUB + X, E), lo_c, masked(there(1, 0), rc[s * 9 + sslot, 8:16, :]))
        groups = X // SUB
        for g in range(groups + 2):
            dx, r = (-1, groups - 1) if g == 0 else (1, 0) if g == groups + 1 else (0, g - 1)
            ha, hq = halo(s, dx, r)
            aext[s, hi_c, g * SUB:(g + 1) * SUB] = ha
            if s == 0:
                put_q(slice(g * SUB, (g + 1) * SUB), hi_c, hq)
        cc[s] = rc[s * 9 + SLOT[(0, 0)], 0:X, :] / sq
        wc = words(s, SLOT[(0, 0)], X, 0)
        we = words(s, SLOT[(0, 1)], 0, 0)
        ww = words(s, SLOT[(0, -1)], 0, 0)
        wide = jnp.concatenate([wc, jnp.where(lane1 < Y // 2, we, ww)], axis=1)
        wide = jnp.broadcast_to(wide, (PROBES, 2 * Y))
        fy[s * PROBES:(s + 1) * PROBES, :] = (2 * ((wide >> jv) & 1) - 1).astype(F32)
        fyn[s * PROBES:(s + 1) * PROBES, :] = 0.5 * (2 * ((wide >> ((jv + 1) & 31)) & 1) - 1).astype(F32)
        xc = words(s, SLOT[(0, 0)], X, 2)
        xn = words(s, nslot, 0, 2)
        xs = words(s, sslot, 16, 2)
        xw = jnp.where(lane1 < SUB, pltpu.roll(jnp.broadcast_to(xn, (SUB, Y)), (SUB - X) % Y, 1)[0:1],
                       jnp.where(lane1 < SUB + X, pltpu.roll(jnp.broadcast_to(xc, (SUB, Y)), SUB, 1)[0:1],
                                 pltpu.roll(jnp.broadcast_to(xs, (SUB, Y)), SUB + X, 1)[0:1]))
        sxw[s] = jnp.transpose(jnp.broadcast_to(xw, (Y, Y)))[0:E]

    j8 = lax.broadcasted_iota(jnp.int32, (GROUP, Y), 0)
    lane_g = lax.broadcasted_iota(jnp.int32, (GROUP, Y), 1)
    first_lane = lane_g == 0
    last_lane = lane_g == Y - 1

    def sides(m, h):
        ml, hl = pltpu.roll(m, 1, 1), pltpu.roll(h, 1, 1)
        mr, hr = pltpu.roll(m, Y - 1, 1), pltpu.roll(h, Y - 1, 1)
        return (jnp.where(first_lane, hl, ml) + jnp.where(last_lane, hr, mr),
                jnp.where(first_lane, ml, hl) + jnp.where(last_lane, mr, hr))

    def bc(ref, row, cols):
        return jnp.broadcast_to(ref[cols, pl.ds(row, 1), :], (GROUP, Y))

    def group(s, k):
        j0 = k * GROUP
        ja = j8 + j0
        jb = (ja + 1) & 31
        d0 = pl.multiple_of(s * PROBES + j0, GROUP)
        fyv = [fy[pl.ds(d0, GROUP), c * Y:(c + 1) * Y] for c in (lo_c, hi_c)]
        fynv = [fyn[pl.ds(d0, GROUP), c * Y:(c + 1) * Y] for c in (lo_c, hi_c)]

        def row(store, e, carry):
            wv = jnp.broadcast_to(sxw[s, pl.ds(e, 1), :], (GROUP, Y))
            fx = (2 * ((wv >> ja) & 1) - 1).astype(F32)
            fxn = (2 * ((wv >> jb) & 1) - 1).astype(F32)
            cur = tuple(
                jnp.broadcast_to(aext[s, c, pl.ds(e, 1), :], (GROUP, Y)) * (fx * fyv[n] + fxn * fynv[n])
                for n, c in enumerate((lo_c, hi_c)))
            new = []
            for t in range(STEPS):
                older, prev = carry[t]
                new.append((prev, cur))
                at = e - 1 - t
                sd = sides(*prev)
                cur = tuple(
                    bc(pext, at, c) * prev[n] + bc(qext, at, c) * (older[n] + cur[n] + sd[n])
                    for n, c in enumerate((lo_c, hi_c)))
            if store:
                i = e - STEPS - SUB
                rbuf[i, pl.ds(d0, GROUP), :] = cur[0] * jnp.broadcast_to(cc[s, pl.ds(i, 1), :], (GROUP, Y))
            return tuple(new)

        zero = fyv[0] * 0.0
        carry = tuple(((zero, zero), (zero, zero)) for _ in range(STEPS))
        begin = SUB - STEPS
        for e in range(begin, begin + 2 * STEPS):
            carry = row(False, e, carry)

        def rows(r, carry):
            for u in range(UNROLL):
                carry = row(True, r * UNROLL + (begin + 2 * STEPS + u), carry)
            return carry

        lax.fori_loop(0, X // UNROLL, rows, carry)

    for s in range(S):
        @pl.loop(0, PROBES // GROUP)
        def _(k):
            group(s, k)

    def inner(i, acc):
        x = jnp.concatenate([rbuf[2 * i], rbuf[2 * i + 1]], axis=1)
        hi = x.astype(BF16)
        lo = (x - hi.astype(F32)).astype(BF16)
        both = jnp.concatenate([hi, lo], axis=0)
        xb[i] = both
        new = lax.dot_general(both, both, (((1,), (1,)), ((), ())), preferred_element_type=F32)
        return new if acc is None else acc + new

    acc = lax.fori_loop(0, X // 2 - 1, lambda i, acc: inner(i + 1, acc), inner(0, None))
    acc = acc[0:D] + acc[D:2 * D]
    fold = 2 * D == Y
    if fold:
        acc = acc + pltpu.roll(acc, D, 1)
        lane_h = lax.broadcasted_iota(jnp.int32, (D // 2, Y), 1)
        gram = jnp.where(lane_h < D, acc[0:D // 2], acc[D // 2:D])
    else:
        gram = acc[:, 0:D] + acc[:, D:2 * D]

    def add_up(buf, mine, n, val, ssem, rsem, dest):
        buf[mine] = val

        def cp(to, slot):
            return pltpu.make_async_remote_copy(
                src_ref=buf.at[mine], dst_ref=buf.at[slot], send_sem=ssem.at[to],
                recv_sem=rsem.at[slot], device_id=dest(to), device_id_type=MESH)

        for to in range(n):
            pl.when(mine != to)(lambda: cp(to, mine).start())
        for frm in range(n):
            pl.when(mine != frm)(lambda: cp(frm, frm).wait_recv())
        for to in range(n):
            pl.when(mine != to)(lambda: cp(to, mine).wait_send())
        total = buf[0]
        for k in range(1, n):
            total = total + buf[k]
        return total

    gram = add_up(gx, mx, NX, gram, gxs, gxr, lambda k: (md, jnp.int32(k), my))
    gram = add_up(gy, my, NY, gram, gys, gyr, lambda k: (md, mx, jnp.int32(k)))

    wide_d = 2 * D
    la = lax.broadcasted_iota(jnp.int32, (D, wide_d), 1)
    ra = lax.broadcasted_iota(jnp.int32, (D, wide_d), 0)
    eye = (la == ra + D).astype(F32)
    if fold:
        full = jnp.concatenate([gram, pltpu.roll(gram, D, 1)], axis=0)
    else:
        full = jnp.concatenate([gram, gram], axis=1)
    mat = jnp.where(la < D, full, eye)
    sub8 = lax.broadcasted_iota(jnp.int32, (SUB, wide_d), 0)
    blocks = D // SUB
    for b in range(blocks):
        panel = mat[0:SUB]
        for t in range(SUB):
            prow = jnp.broadcast_to(panel[t:t + 1, :], (SUB, wide_d))
            col = b * SUB + t
            scale = lax.rsqrt(prow[:, col:col + 1])
            prow = prow * scale
            mult = panel[:, col:col + 1] * scale
            panel = jnp.where(sub8 == t, prow, jnp.where(sub8 > t, panel - mult * prow, panel))
        aug[b * SUB:(b + 1) * SUB, :] = panel
        if b + 1 < blocks:
            lhs = panel[:, 0:D]
            upd = lax.dot_general(lhs, panel, (((0,), (0,)), ((), ())), precision=HIGH,
                                  preferred_element_type=F32)
            mat = mat[SUB:] - upd[(b + 1) * SUB:]

    root = math.sqrt(X * Y * NX * NY)
    own = aug[pl.ds(pl.multiple_of(md * PROBES, PROBES), PROBES), :]
    lano = lax.broadcasted_iota(jnp.int32, own.shape, 1)
    orow = lax.broadcasted_iota(jnp.int32, own.shape, 0) + md * PROBES
    upper = jnp.where(lano >= orow, own, 0.0)
    fac_ref[...] = upper[:, 0:D] * (1.0 / root)
    linv = own[:, D:2 * D] * root
    l2 = jnp.concatenate([linv, linv], axis=1)
    l2h = l2.astype(BF16)
    l2l = (l2 - l2h.astype(F32)).astype(BF16)
    left = jnp.concatenate([l2h, l2l], axis=0)

    def final(i):
        y = lax.dot_general(left, xb[i], (((1,), (0,)), ((), ())), preferred_element_type=F32)
        y = y[0:PROBES] + y[PROBES:2 * PROBES]
        out_ref[:, 2 * i, :] = y[:, 0:Y]
        out_ref[:, 2 * i + 1, :] = y[:, Y:2 * Y]

    pl.loop(0, X // 2)(final)


def solution(mesh):
    S, NX, NY = (mesh.shape[k] for k in ("dir", "sx", "sy"))

    def shards(signs_x, signs_y, heights, velocity, background):
        X, Y = heights.shape
        D = S * PROBES
        E = X + 2 * SUB
        gshape = (D // 2, Y) if 2 * D == Y else (D, D)
        vm = pl.BlockSpec(memory_space=pltpu.VMEM)
        dma = pltpu.SemaphoreType.DMA
        return pl.pallas_call(
            functools.partial(kernel, S, NX, NY, X, Y),
            out_shape=(jax.ShapeDtypeStruct((PROBES, X, Y), F32), jax.ShapeDtypeStruct((PROBES, D), F32)),
            in_specs=[vm] * 5,
            out_specs=(vm, vm),
            scratch_shapes=[
                pltpu.VMEM((X + 56, Y), F32),
                pltpu.VMEM((S * 9, X + 8, Y), F32),
                pltpu.VMEM((S, 2, E, Y), F32),
                pltpu.VMEM((2, E, Y), F32),
                pltpu.VMEM((2, E, Y), F32),
                pltpu.VMEM((S, X, Y), F32),
                pltpu.VMEM((S, E, Y), jnp.int32),
                pltpu.VMEM((D, 2 * Y), F32),
                pltpu.VMEM((D, 2 * Y), F32),
                pltpu.VMEM((X, D, Y), F32),
                pltpu.VMEM((X // 2, 2 * D, 2 * Y), BF16),
                pltpu.VMEM((NX,) + gshape, F32),
                pltpu.VMEM((NY,) + gshape, F32),
                pltpu.VMEM((D, 2 * D), F32),
                dma((S * 9,)), dma((S * 9,)),
                dma((NX,)), dma((NX,)), dma((NY,)), dma((NY,)),
            ],
            compiler_params=pltpu.CompilerParams(
                collective_id=0, has_side_effects=True, vmem_limit_bytes=56 * 1024 * 1024),
        )(signs_x, signs_y, heights, velocity, background)

    in_specs = (P("dir", "sx"), P("dir", "sy"), P("sx", "sy"), P("sx", "sy"), P("dir", "sx", "sy"))
    out_specs = (P("dir", "sx", "sy"), P("dir", None))
    return jax.shard_map(shards, mesh=mesh, in_specs=in_specs, out_specs=out_specs, check_vma=False)
```

time: 232 us -> 60.7 us (0.26)
  blocking collectives: 61.3 us -> 0 us
  Pallas kernels: 0 us -> 56.9 us
  starting transfers between devices: 46.5 us -> 0 us
  waiting for transfers between devices: 43.9 us -> 0 us
  other arithmetic: 28.4 us -> 0 us
  local copies, waits for them, and re-layouts: 30.7 us -> 2.92 us
  between operations: 14.4 us -> 0.65 us
  matrix products: 6.09 us -> 0 us
    psum x1 -> x0, blocking collectives: 61.3 us -> none  [shards(): gram_matrix = lax.psum(local_gram, ('sx', 'sy'))]
    pallas_call x0 -> x1, Pallas kernels: none -> 56.9 us  [shards(): pl.pallas_call(functools.partial(kernel, S, NX, NY, X, Y), out_shape=(jax...]
    ppermute x16 -> x0, starting transfers between devices: 46.5 us -> none  [the longest x8 36.2 us: with_halo(): lax.ppermute(tail, axis, [(i, (i + 1) % count) for i in range(ends)])]
    all_gather x1 -> x0, waiting for transfers between devices: 39.8 us -> none  [shards(): all_rows = lax.all_gather(response, 'dir', axis=0, tiled=True)]
    slice x18 -> x0, local copies, waits for them, and re-layouts: 15.4 us -> none  [the longest x8 11.2 us: with_halo(): head = lax.slice_in_dim(cells, 0, width, axis=dim)]
    ppermute x8 -> x0, local copies, waits for them, and re-layouts: 12.8 us -> none  [the longest x4 7.68 us: with_halo(): lax.ppermute(tail, axis, [(i, (i + 1) % count) for i in range(ends)])]
    another operation x5 -> x0, other arithmetic: 12.1 us -> none  [the longest x3 6.52 us: shards(): factor_low = jnp.linalg.cholesky(gram_matrix)]
    mul x6 -> x0, other arithmetic: 11.4 us -> none  [the longest x4 11 us: apply_step(): weighted = stiffness * wavefield]
  transfers between devices with their start and end apart: 17 -> 0, of which waited for: 8 -> 0; matrix products, arithmetic and copies ran while one was open for 4% -> 0% of each run, Pallas kernels for 0% -> 0%
where the time goes in v1:
time: 60.7 us; the launch traced here: 60.5 us
  Pallas kernels  56.9 us (94%)
  local copies, waits for them, and re-layouts  2.92 us (5%)
  between operations  0.65 us (1%)
    pallas_call x1, Pallas kernels, shards(): pl.pallas_call(functools.partial(kernel, S, NX, NY, X, Y), out_shape=(jax...  56.9 us
    unnamed x4, local copies, waits for them, and re-layouts  2.92 us

profile of v1, /device:TPU:0, one launch (start us, length us, event | category | flops | bytes accessed | tf_op | source)
XLA Modules:
  0.0 60.5 jit_solution(4289786160490454713)
XLA Ops:
  0.6 56.9 %shard_map.68 = (f32[32,64,128]{2,1,0:T(8,128)}, f32[32,64]{1,0:T(8,128)}) custom-call(s32[1,64]{1,0:T(1,128)} %sx_ref.1, s32[1,128]{1,0:T(1,128)} %sy_ref.1, s32[64,128]{1,0:T(8,128)} %h_ref.1, f32[64,128]{1,0:T(8,128)} %v_ref.1, f32[1,64,128]{2,1,0:T(8,128)} %b_ref.1), custom_call_target="tpu_custom_call" | custom-call | tf_op jit(solution)/shard_map/pallas_call | solution.py:369
  57.5 0.0 copy-start
  57.5 2.3 %copy.9 = f32[32,64,128]{2,1,0:T(8,128)} copy(f32[32,64,128]{2,1,0:T(8,128)} %get-tuple-element.4) | data formatting | bytes 2097152
  59.8 0.0 copy-done
  59.8 0.6 %copy.10 = f32[32,64]{1,0:T(8,128)} copy(f32[32,64]{1,0:T(8,128)S(1)} %copy-done) | data formatting | bytes 16384
Async XLA Ops:
  57.5 2.3 %copy-start = (f32[32,64]{1,0:T(8,128)S(1)}, f32[32,64]{1,0:T(8,128)}, u32[]{:S(2)}) copy-start(f32[32,64]{1,0:T(8,128)} %get-tuple-element.5) | copy-start | bytes 24580

commit v2 on v1

--- a/solution.py
+++ b/solution.py
@@ -13,8 +13,8 @@
 TAU = 0.02
 STEPS = 4
 SUB = 8
-GROUP = 16
-UNROLL = 4
+GROUP = 32
+UNROLL = 8
 MESH = pl.DeviceIdType.MESH
 OFFS = [(dx, dy) for dx in (-1, 0, 1) for dy in (-1, 0, 1)]
 SLOT = {o: n for n, o in enumerate(OFFS)}
@@ -276,7 +276,14 @@
         new = lax.dot_general(both, both, (((1,), (1,)), ((), ())), preferred_element_type=F32)
         return new if acc is None else acc + new
 
-    acc = lax.fori_loop(0, X // 2 - 1, lambda i, acc: inner(i + 1, acc), inner(0, None))
+    per = 4
+
+    def several(i, acc):
+        for u in range(per):
+            acc = inner(i * per + u, acc)
+        return acc
+
+    acc = lax.fori_loop(0, X // 2 // per - 1, lambda i, acc: several(i + 1, acc), several(0, None))
     acc = acc[0:D] + acc[D:2 * D]
     fold = 2 * D == Y
     if fold:
@@ -353,7 +360,7 @@
         out_ref[:, 2 * i, :] = y[:, 0:Y]
         out_ref[:, 2 * i + 1, :] = y[:, Y:2 * Y]
 
-    pl.loop(0, X // 2)(final)
+    pl.loop(0, X // 2, unroll=8)(final)
 
 
 def solution(mesh):

time: 60.7 us -> 42.8 us (0.71)
  Pallas kernels: 56.9 us -> 39 us
    pallas_call x1, Pallas kernels: 56.9 us -> 39 us  [shards(): pl.pallas_call(functools.partial(kernel, S, NX, NY, X, Y), out_shape=(jax...]
where the time goes in v2:
time: 42.8 us; the launch traced here: 42.5 us
  Pallas kernels  39 us (91%)
  local copies, waits for them, and re-layouts  2.92 us (7%)
  between operations  0.65 us (2%)
    pallas_call x1, Pallas kernels, shards(): pl.pallas_call(functools.partial(kernel, S, NX, NY, X, Y), out_shape=(jax...  39 us
    unnamed x4, local copies, waits for them, and re-layouts  2.92 us

profile of v2, /device:TPU:0, one launch (start us, length us, event | category | flops | bytes accessed | tf_op | source)
XLA Modules:
  0.0 42.5 jit_solution(5663394139399899779)
XLA Ops:
  0.6 39.0 %shard_map.68 = (f32[32,64,128]{2,1,0:T(8,128)}, f32[32,64]{1,0:T(8,128)}) custom-call(s32[1,64]{1,0:T(1,128)} %sx_ref.1, s32[1,128]{1,0:T(1,128)} %sy_ref.1, s32[64,128]{1,0:T(8,128)} %h_ref.1, f32[64,128]{1,0:T(8,128)} %v_ref.1, f32[1,64,128]{2,1,0:T(8,128)} %b_ref.1), custom_call_target="tpu_custom_call" | custom-call | tf_op jit(solution)/shard_map/pallas_call | solution.py:376
  39.6 0.0 copy-start
  39.6 2.3 %copy.9 = f32[32,64,128]{2,1,0:T(8,128)} copy(f32[32,64,128]{2,1,0:T(8,128)} %get-tuple-element.4) | data formatting | bytes 2097152
  41.9 0.0 copy-done
  41.9 0.6 %copy.10 = f32[32,64]{1,0:T(8,128)} copy(f32[32,64]{1,0:T(8,128)S(1)} %copy-done) | data formatting | bytes 16384
Async XLA Ops:
  39.6 2.3 %copy-start = (f32[32,64]{1,0:T(8,128)S(1)}, f32[32,64]{1,0:T(8,128)}, u32[]{:S(2)}) copy-start(f32[32,64]{1,0:T(8,128)} %get-tuple-element.5) | copy-start | bytes 24580
